TPU v7x, 32 devices: a whole 2x2x4 slice. The times are simulated.
32 devices in a mesh: seq: 16 (over z, y, core), head: 2 (over x).
Axes of the slice: x: 2, y: 2, z: 4, core: 2. Of those that a mesh axis runs over, the one named last changes fastest.
Arguments:
- latent_queries: bfloat16 [2048, 128, 576], P('seq', 'head'), may hold values from -16 to 16
- latent_keys: bfloat16 [1024, 576], P('seq'), may hold values from -6 to 6
- index_queries: bfloat16 [2048, 64, 128], P('seq', 'head'), may hold values from -8 to 8
- index_keys: bfloat16 [1024, 128], P('seq'), may hold values from -6 to 6
- head_weights: float32 [2048, 64], P('seq', 'head'), may hold values from -18 to 18
- visible: int32 [2048], P('seq'), may hold values from 1 to 1024, as said below
Outputs:
- grad_index_queries: bfloat16 [2048, 64, 128], P('seq', 'head')
- grad_head_weights: float32 [2048, 64], P('seq', 'head')
- grad_index_keys: float32 [1024, 128], P('seq')
Inputs may be any that keep to these rules, and one draw needn't show every extreme that they name: Row t sees keys 0 to visible[t] - 1, never more than (t * 1024) // 2048 + 1 of them; the last row sees all 1024 keys.
All inputs are finite; a program needn't handle non-finite values.
Results may differ from a plain program's by a relative error of at most 0.0049.
Values may be sent and summed in bfloat16 or wider, within the bound.
A program may use at most 128 MiB of HBM per device.

v0:
```python
import jax
import jax.numpy as jnp
from jax import lax
from jax.sharding import PartitionSpec as P

MLA_HEADS = 128
INDEX_HEADS = 64


mla_scale = 192.0 ** (-0.5)
loss_weight = 16.0
neg_fill = -1e30
start_peak = -5e29


def latent_scores(queries, portion, visible):
    row_count, head_count, width = queries.shape
    flat = queries.reshape(row_count * head_count, width)
    scores = (
        lax.dot_general(portion, flat, (((1,), (1,)), ((), ())), preferred_element_type=jnp.float32)
        * mla_scale
    )
    key_ids = lax.broadcasted_iota(jnp.int32, (portion.shape[0], 1), 0)
    limit = jnp.broadcast_to(visible[:, None], (row_count, head_count)).reshape(
        1, row_count * head_count
    )
    return jnp.where(key_ids < limit, scores, neg_fill)


def stats_update(status, queries, portion, visible):
    maxima, totals = status
    row_count, head_count = maxima.shape
    scores = latent_scores(queries, portion, visible)
    old_max = maxima.reshape(row_count * head_count)
    new_max = jnp.maximum(old_max, jnp.max(scores, axis=0))
    new_total = jnp.sum(jnp.exp(scores - new_max[None, :]), axis=0)
    return (new_max.reshape(row_count, head_count), new_total.reshape(row_count, head_count))


def target_update(queries, portion, visible, normalizer):
    row_count, head_count = normalizer.shape
    key_count = portion.shape[0]
    scores = latent_scores(queries, portion, visible)
    probs = jnp.exp(scores - normalizer.reshape(1, row_count * head_count))
    summed = jnp.sum(probs.reshape(key_count, row_count, head_count), axis=2)
    return summed.T / MLA_HEADS


def index_logits(index_queries, index_all, head_weights, span):
    row_count = index_queries.shape[0]
    key_count = index_all.shape[0]
    dot_scale = index_queries.shape[2] ** (-0.5)
    head_scale = INDEX_HEADS ** (-0.5)

    def one_span(number, logits):
        offset = number * span
        portion = lax.dynamic_slice_in_dim(index_all, offset, span, 0)
        products = (
            jnp.einsum("thd,kd->thk", index_queries, portion, preferred_element_type=jnp.float32)
            * dot_scale
        )
        summed = jnp.sum(head_weights[:, :, None] * jnp.maximum(products, 0.0), axis=1) * head_scale
        return lax.dynamic_update_slice_in_dim(logits, summed, offset, 1)

    return lax.fori_loop(
        0, key_count // span, one_span, jnp.zeros((row_count, key_count), jnp.float32)
    )


def index_backward(index_queries, index_all, head_weights, row_grad, span):
    row_count, head_count, depth = index_queries.shape
    key_count = index_all.shape[0]
    dot_scale = depth ** (-0.5)
    head_scale = INDEX_HEADS ** (-0.5)
    weighted = head_weights * head_scale

    def one_span(number, running):
        query_grad, weight_grad, key_grad = running
        offset = number * span
        portion = lax.dynamic_slice_in_dim(index_all, offset, span, 0)
        slope = lax.dynamic_slice_in_dim(row_grad, offset, span, 1)
        products = (
            jnp.einsum("thd,kd->thk", index_queries, portion, preferred_element_type=jnp.float32)
            * dot_scale
        )
        edge_grad = jnp.where(products > 0.0, slope[:, None, :] * weighted[:, :, None], 0.0).astype(
            jnp.bfloat16
        )
        query_grad = query_grad + jnp.einsum(
            "thk,kd->thd", edge_grad, portion, preferred_element_type=jnp.float32
        )
        weight_grad = weight_grad + jnp.sum(slope[:, None, :] * jnp.maximum(products, 0.0), axis=2)
        key_term = jnp.einsum(
            "thk,thd->kd", edge_grad, index_queries, preferred_element_type=jnp.float32
        )
        key_grad = lax.dynamic_update_slice_in_dim(key_grad, key_term, offset, 0)
        return (query_grad, weight_grad, key_grad)

    initial = (
        jnp.zeros((row_count, head_count, depth), jnp.float32),
        jnp.zeros((row_count, head_count), jnp.float32),
        jnp.zeros((key_count, depth), jnp.float32),
    )
    query_grad, weight_grad, key_grad = lax.fori_loop(0, key_count // span, one_span, initial)
    return (
        (query_grad * dot_scale).astype(jnp.bfloat16),
        weight_grad * head_scale,
        key_grad * dot_scale,
    )


def body(latent_queries, latent_keys, index_queries, index_keys, head_weights, visible):
    row_count = latent_queries.shape[0]
    head_count = latent_queries.shape[1]
    key_count = latent_keys.shape[0] * lax.axis_size("seq")
    span = min(512, key_count)
    initial = (
        jnp.full((row_count, head_count), start_peak, jnp.float32),
        jnp.zeros((row_count, head_count), jnp.float32),
    )
    status = initial
    status = stats_update(
        status, latent_queries, lax.all_gather(latent_keys, "seq", axis=0, tiled=True), visible
    )
    collected = lax.all_gather(index_keys, "seq", axis=0, tiled=True)
    status, index_all = (status, collected)
    normalizer = status[0] + jnp.log(status[1])
    logit_part = index_logits(index_queries, index_all, head_weights, span)
    target_part = target_update(
        latent_queries, lax.all_gather(latent_keys, "seq", axis=0, tiled=True), visible, normalizer
    )
    target_share, logit_share = (
        lax.psum_scatter(target_part, "head", scatter_dimension=1, tiled=True),
        lax.psum_scatter(logit_part, "head", scatter_dimension=1, tiled=True),
    )
    share_width = logit_share.shape[1]
    columns = lax.axis_index("head") * share_width + lax.broadcasted_iota(
        jnp.int32, (1, share_width), 1
    )
    logit_share = jnp.where(columns < visible[:, None], logit_share, neg_fill)
    row_peak = lax.pmax(jnp.max(logit_share, axis=1), "head")
    weights = jnp.exp(logit_share - row_peak[:, None])
    row_sum = lax.psum(jnp.sum(weights, axis=1), "head")
    grad_share = loss_weight * (weights / row_sum[:, None] - target_share)
    row_grad = lax.all_gather(grad_share, "head", axis=1, tiled=True)
    query_grad, weight_grad, key_term = index_backward(
        index_queries, index_all, head_weights, row_grad, span
    )
    owned = lax.psum_scatter(key_term, "seq", scatter_dimension=0, tiled=True)
    key_grad = lax.psum(owned, "head")
    return (query_grad, weight_grad, key_grad)


def solution(mesh):
    placed = (
        P("seq", "head", None),
        P("seq", None),
        P("seq", "head", None),
        P("seq", None),
        P("seq", "head"),
        P("seq"),
    )
    return jax.shard_map(
        body,
        mesh=mesh,
        in_specs=placed,
        out_specs=(P("seq", "head", None), P("seq", "head"), P("seq", None)),
        check_vma=False,
    )
```

profile of v0, /device:TPU:0, one launch (start us, length us, event | category | flops | bytes accessed | tf_op | source)
XLA Modules:
  0.0 280.2 jit_solution(3439737571994594935)
XLA Ops:
  8.0 0.0 all-gather.2.cloned.1.call-start
  8.0 0.7 all-gather.2.cloned.1.call-update
  8.7 0.0 reduce-scatter.4.cloned.1.call-start
  8.8 1.6 copy.28
  10.4 24.2 %all_gather.10 = bf16[1024,128]{1,0:T(8,128)(2,1)S(1)} all-gather(bf16[64,128]{1,0:T(8,128)(2,1)} %param.13), channel_id=1, replica_groups=mesh['seq'=16,'head'=2] {'seq'}, dimensions={0}, use_global_device_ids=true | all-gather | bytes 278528 | tf_op jit(solution)/shard_map/all_gather | solution.py:125
  34.7 0.0 copy-start.4
  34.7 4.5 %while.31 = (s32[]{:T(128)}, f32[128,1024]{1,0:T(8,128)S(1)}, f32[128,32]{0,1:T(8,128)}, bf16[1024,128]{1,0:T(8,128)(2,1)S(1)}, bf16[128,32,128]{2,0,1:T(8,128)(...) while((s32[]{:T(128)}, f32[128,1024]{1,0:T(8,128)S(1)}, f32[128,32]{0,1:T(8,128)}, ...), condition=%wide.region_2.3_spmd, body=%wide.region_0.0_spmd.sunk | while | flops 545259520 | bytes 3031187 | solution.py:65
  34.7 2.0 multiply_reduce_fusion.2
  36.8 0.1 copy.43
  36.9 2.0 multiply_reduce_fusion.2
  39.0 0.1 copy.43
  39.2 0.8 copy-done.2
  40.0 0.0 reduce-scatter.4.cloned.1.call-update
  40.0 0.2 reduce-scatter.6.cloned.1.call-start
  40.2 0.1 broadcast_in_dim.52
  40.3 0.1 lt.66
  40.4 14.9 %copy.26 = bf16[128,64,576]{2,1,0:T(8,128)(2,1)} copy(bf16[128,64,576]{0,2,1:T(8,128)(2,1)} %param.10) | data formatting | bytes 18874368 | tf_op args[0]
  55.2 23.2 %fusion.12 = (f32[8192]{0:T(1024)S(1)}, f32[1024,8192]{1,0:T(8,128)}) fusion(s32[8192]{0:T(1024)S(1)} %lt.66, bf16[1024,576]{1,0:T(8,128)(2,1)} %all-gather.2.cloned.1.call-done, bf16[8192,576]{1,0:T(8,128)(2,1)} %bitcast.56), kind=kOutput, calls=%fused_computation.26 | convolution fusion | flops 9697222656 | bytes 44236800 | tf_op jit(solution)/shard_map/dot_general | solution.py:20
  78.4 15.8 %exponential_reduce_fusion = f32[8192]{0:T(1024)S(1)} fusion(f32[1024,8192]{1,0:T(8,128)} %get-tuple-element.337, f32[8192]{0:T(1024)S(1)} %broadcast_maximum_fusion, s32[8192]{0:T(1024)S(1)} %lt.66), kind=kLoop, calls=%fused_computation.23 | loop fusion | flops 41934848 | bytes 33652736 | tf_op jit(solution)/shard_map/reduce_sum | solution.py:36
  94.3 4.4 %copy-done.1 = f32[1024,8192]{1,0:T(8,128)S(1)} copy-done((f32[1024,8192]{1,0:T(8,128)S(1)}, f32[1024,8192]{1,0:T(8,128)}, u32[]{:S(2)}) %copy-start.1) | copy-done | bytes 33554456
  98.6 12.5 %subtract_exponential_fusion = f32[1024,8192]{1,0:T(8,128)} fusion(f32[1024,8192]{1,0:T(8,128)S(1)} %copy-done.1, f32[8192]{0:T(1024)S(1)} %log_add_fusion, s32[8192]{0:T(1024)S(1)} %lt.66), kind=kLoop, calls=%fused_computation.22 | loop fusion | flops 33554432 | bytes 67174400 | tf_op jit(solution)/shard_map/exp | solution.py:44
  111.2 33.4 %copy.27 = f32[1024,8192]{0,1:T(8,128)} copy(f32[1024,8192]{1,0:T(8,128)} %subtract_exponential_fusion) | data formatting | bytes 67108864 | tf_op jit(solution)/shard_map/exp | solution.py:44
  144.6 13.1 %bitcast_reduce_fusion = f32[1024,128]{0,1:T(8,128)S(1)} fusion(f32[1024,8192]{0,1:T(8,128)} %copy.27), kind=kLoop, calls=%fused_computation.21 | loop fusion | flops 8257536 | bytes 34078720 | tf_op jit(solution)/shard_map/reduce_sum | solution.py:45
  157.7 0.8 multiply_bitcast_fusion.1
  158.5 0.0 reduce-scatter.6.cloned.1.call-update
  158.5 0.0 reduce-scatter.8.cloned.1.call-start
  158.6 0.0 reduce-scatter.4.cloned.1.call-done
  158.7 1.1 fusion.14
  159.8 4.9 %pmax.7 = f32[128]{0:T(128)S(1)} all-reduce(f32[128]{0:T(128)S(1)} %fusion.14), channel_id=1, replica_groups=mesh['seq'=16,'head'=2] {'head'}, use_global_device_ids=true, to_apply=%region_5.6 | all-reduce | flops 128 | bytes 1024 | tf_op jit(solution)/shard_map/pmax | solution.py:141
  164.7 1.1 fusion.15
  165.9 4.9 %psum.14 = f32[128]{0:T(128)S(1)} all-reduce(f32[128]{0:T(128)S(1)} %fusion.15), channel_id=1, replica_groups=mesh['seq'=16,'head'=2] {'head'}, use_global_device_ids=true, to_apply=%region_7.8 | all-reduce | flops 128 | bytes 1024 | tf_op jit(solution)/shard_map/psum | solution.py:143
  170.8 1.2 subtract_multiply_fusion
  172.0 8.4 %all_gather.12 = f32[128,1024]{1,0:T(8,128)S(1)} all-gather(f32[128,512]{1,0:T(8,128)S(1)} %subtract_multiply_fusion), channel_id=1, replica_groups=mesh['seq'=16,'head'=2] {'head'}, dimensions={1}, use_global_device_ids=true | all-gather | bytes 786432 | tf_op jit(solution)/shard_map/all_gather | solution.py:145
  180.5 25.5 %while.32 = (s32[]{:T(128)}, f32[128,32,128]{2,0,1:T(8,128)}, f32[128,32]{0,1:T(8,128)S(1)}, f32[1024,128]{1,0:T(8,128)S(1)}, bf16[1024,128]{1,0:T(8,128)(2,1)S(...) while((s32[]{:T(128)}, f32[128,32,128]{2,0,1:T(8,128)}, ...), condition=%wide.region_14.15_spmd.clone, body=%wide.region_12.14_spmd.clone.sunk | while | flops 1641025536 | bytes 67469528 | solution.py:104
  180.5 0.1 copy.44
  180.7 4.5 %fusion.33 = (f32[128,32]{0,1:T(8,128)S(1)}, f32[512,128,32]{1,0,2:T(8,128)}) fusion(f32[128,512]{0,1:T(8,128)S(1)} %copy.44, bf16[128,32,128]{2,0,1:T(8,128)(2,1)S(1)} %get-tuple-element.478, bf16[1024,128]{1,0:T(8,128)(2,1)S(1)} %get-tuple-element.477, s32[]{:T(128)S(6)} %select_n.64), kind=kOutput, calls=%fused_computation.7.clone.1 | convolution fusion | flops 545255424 | bytes 9846788 | tf_op jit(solution)/shard_map/while/body/eval_jaxpr/thd,kd->thk/dot_general | solution.py:83
  185.2 6.5 %select_add_fusion.4 = f32[128,32,128]{2,0,1:T(8,128)} fusion(f32[128,32,128]{2,0,1:T(8,128)} %get-tuple-element.462, pred[]{:T(512)S(6)} %compare.3, bf16[1024,128]{1,0:T(8,128)(2,1)S(1)} %get-tuple-element.477, s32[]{:T(128)S(6)} %select_n.64, f32[512,128,32]{1,0,2:T(8,128)} %get-tuple-element.420, f32[128,32]{0,1:T(8,128)S(1)} %get-tuple-element.480, ...), kind=kOutput, calls=%fused_computation.9.clone.1 | convolution fusion | flops 548405248 | bytes 12992517 | tf_op jit(solution)/shard_map/while/body/eval_jaxpr/thk,kd->thd/dot_general | solution.py:89
  191.7 1.3 fusion.34
  193.0 0.1 copy.44
  193.1 4.5 %fusion.33 = (f32[128,32]{0,1:T(8,128)S(1)}, f32[512,128,32]{1,0,2:T(8,128)}) fusion(f32[128,512]{0,1:T(8,128)S(1)} %copy.44, bf16[128,32,128]{2,0,1:T(8,128)(2,1)S(1)} %get-tuple-element.478, bf16[1024,128]{1,0:T(8,128)(2,1)S(1)} %get-tuple-element.477, s32[]{:T(128)S(6)} %select_n.64), kind=kOutput, calls=%fused_computation.7.clone.1 | convolution fusion | flops 545255424 | bytes 9846788 | tf_op jit(solution)/shard_map/while/body/eval_jaxpr/thd,kd->thk/dot_general | solution.py:83
  197.6 7.1 %select_add_fusion.4 = f32[128,32,128]{2,0,1:T(8,128)} fusion(f32[128,32,128]{2,0,1:T(8,128)} %get-tuple-element.462, pred[]{:T(512)S(6)} %compare.3, bf16[1024,128]{1,0:T(8,128)(2,1)S(1)} %get-tuple-element.477, s32[]{:T(128)S(6)} %select_n.64, f32[512,128,32]{1,0,2:T(8,128)} %get-tuple-element.420, f32[128,32]{0,1:T(8,128)S(1)} %get-tuple-element.480, ...), kind=kOutput, calls=%fused_computation.9.clone.1 | convolution fusion | flops 548405248 | bytes 12992517 | tf_op jit(solution)/shard_map/while/body/eval_jaxpr/thk,kd->thd/dot_general | solution.py:89
  204.8 1.3 fusion.34
  206.0 0.8 broadcast_multiply_fusion
  206.9 0.0 reduce-scatter.8.cloned.1.call-update
  206.9 0.6 broadcast_multiply_fusion.1
  207.5 3.9 %fusion.13 = bf16[128,32,128]{2,1,0:T(8,128)(2,1)} fusion(f32[128,32,128]{2,0,1:T(8,128)} %get-tuple-element.239), kind=kLoop, calls=%fused_computation.28 | loop fusion | flops 1048576 | bytes 3145728 | tf_op jit(solution)/shard_map/convert_element_type | solution.py:106
  211.4 51.8 %reduce-scatter.8.cloned.1.call-done = f32[64,128]{1,0:T(8,128)} async-done(((f32[1024,128]{1,0:T(8,128)}), f32[64,128]{1,0:T(8,128)}) %reduce-scatter.8.cloned.1.call-update) | async-done | bytes 32784 | tf_op jit(solution)/shard_map/reduce_scatter | solution.py:149
  263.2 9.5 %psum.15 = f32[64,128]{1,0:T(8,128)} all-reduce(f32[64,128]{1,0:T(8,128)} %reduce-scatter.8.cloned.1.call-done), channel_id=1, replica_groups=mesh['seq'=16,'head'=2] {'head'}, use_global_device_ids=true, to_apply=%region_16.17 | all-reduce | flops 8192 | bytes 65536 | tf_op jit(solution)/shard_map/psum | solution.py:150
  (27 shorter events, 0.3 us)
Async XLA Ops:
  8.0 47.2 %all-gather.2.cloned.1.call-start = ((), (), s32[]{:S(2)}) async-start(), calls=%async_computation.4 | async-start | bytes 1392640 | tf_op jit(solution)/shard_map/all_gather | solution.py:130
  8.7 149.9 %reduce-scatter.4.cloned.1.call-start = ((), (), s32[]{:S(2)}) async-start(), calls=%async_computation.3 | async-start | bytes 786432 | tf_op jit(solution)/shard_map/reduce_scatter | solution.py:134
  34.7 5.5 %copy-start.4 = (s32[128]{0:T(128)S(1)}, s32[128]{0:T(128)}, u32[]{:S(2)}) copy-start(s32[128]{0:T(128)} %param.15) | copy-start | bytes 1540
  39.2 0.8 copy-start.2
  40.0 130.9 %reduce-scatter.6.cloned.1.call-start = ((), (), s32[]{:S(2)}) async-start(), calls=%async_computation.5 | async-start | bytes 786432 | tf_op jit(solution)/shard_map/reduce_scatter | solution.py:133
  78.4 20.2 %copy-start.1 = (f32[1024,8192]{1,0:T(8,128)S(1)}, f32[1024,8192]{1,0:T(8,128)}, u32[]{:S(2)}) copy-start(f32[1024,8192]{1,0:T(8,128)} %get-tuple-element.337) | copy-start | bytes 100663296
  144.6 14.0 %copy-start.3 = (f32[128,32]{0,1:T(8,128)S(1)}, f32[128,32]{0,1:T(8,128)}, u32[]{:S(2)}) copy-start(f32[128,32]{0,1:T(8,128)} %get-tuple-element.502) | copy-start | bytes 49156
  158.5 104.7 %reduce-scatter.8.cloned.1.call-start = ((), (), s32[]{:S(2)}) async-start(), calls=%async_computation.6 | async-start | bytes 557056 | tf_op jit(solution)/shard_map/reduce_scatter | solution.py:149
  185.2 6.5 %copy-start = (f32[512,128,32]{1,0,2:T(8,128)S(1)}, f32[512,128,32]{1,0,2:T(8,128)}, u32[]{:S(2)}) copy-start(f32[512,128,32]{1,0,2:T(8,128)} %get-tuple-element.420) | copy-start | bytes 25165828 | tf_op jit(solution)/shard_map/while
  197.6 7.1 %copy-start = (f32[512,128,32]{1,0,2:T(8,128)S(1)}, f32[512,128,32]{1,0,2:T(8,128)}, u32[]{:S(2)}) copy-start(f32[512,128,32]{1,0,2:T(8,128)} %get-tuple-element.420) | copy-start | bytes 25165828 | tf_op jit(solution)/shard_map/while
Sparse Core Ops, SparseCore 0:
  11.1 41.5 all-gather.1
  207.0 56.1 reduce-scatter.7
Sparse Core Ops, SparseCore 1:
  40.1 11.8 reduce-scatter.3
  158.6 11.9 reduce-scatter.5
where the time goes:
time: 282 us; the launch traced here: 280 us
  local copies, waits for them, and re-layouts  55.9 us (20%)
  waiting for transfers between devices  52.6 us (19%)
  matrix products  52.3 us (19%)
  blocking collectives  52.1 us (18%)
  other arithmetic  51.1 us (18%)
  between operations  15.6 us (6%)
    reduce_scatter x1, waiting for transfers between devices, body(): owned = lax.psum_scatter(key_term, 'seq', scatter_dimension=0, tiled=True)  51.8 us
    exp x1, local copies, waits for them, and re-layouts, target_update(): probs = jnp.exp(scores - normalizer.reshape(1, row_count * head_count))  33.4 us
    all_gather x1, blocking collectives, body(): collected = lax.all_gather(index_keys, 'seq', axis=0, tiled=True)  24.2 us
    dot_general x1, matrix products, latent_scores(): lax.dot_general(portion, flat, (((1,), (1,)), ((), ())), preferred_elemen...  23.2 us
    unnamed x10, local copies, waits for them, and re-layouts  21.7 us
    reduce_sum x1, other arithmetic, stats_update(): new_total = jnp.sum(jnp.exp(scores - new_max[None, :]), axis=0)  15.8 us
    dot_general x2, matrix products, one_span(): jnp.einsum('thk,kd->thd', edge_grad, portion, preferred_element_type=jnp....  13.6 us
    reduce_sum x1, other arithmetic, target_update(): summed = jnp.sum(probs.reshape(key_count, row_count, head_count), axis=2)  13.1 us
  transfers between devices with their start and end apart: 4, of which 1 were waited for; matrix products, arithmetic and copies ran while one was open for 45% of the time, Pallas kernels for 0%

commit v1 on v0

v1 whole, which is shorter than its diff:
```python
import functools
import jax
import jax.numpy as jnp
from jax import lax
from jax.experimental import pallas as pl
from jax.experimental.pallas import tpu as pltpu
from jax.sharding import PartitionSpec as P

MLA_HEADS = 128
INDEX_HEADS = 64
LOG2E = 1.4426950408889634

mla_scale = 192.0 ** (-0.5)
loss_weight = 16.0
neg_fill = -1e30
MESH = pl.DeviceIdType.MESH
VMEM = pltpu.VMEM


def line_sizes(n):
    ny = 2 if n <= 16 else 4
    return n // (2 * ny), ny


def remote(src, dst, ssem, rsem, device):
    return pltpu.make_async_remote_copy(
        src_ref=src, dst_ref=dst, send_sem=ssem, recv_sem=rsem, device_id=device, device_id_type=MESH
    )


def gather_kernel(n, lat_ref, idx_ref, lat_all, idx_all, lsem, zs, zr, ys, yr, cs, cr):
    nz, ny = line_sizes(n)
    me = lax.axis_index("seq")
    core = me % 2
    y = (me // 2) % ny
    z = me // (2 * ny)
    size = lat_ref.shape[0]

    def at(zz, yy, cc):
        return (zz * ny + yy) * 2 + cc

    zpeers = [(z + k) % nz for k in range(1, nz)]
    ypeers = [(y + k) % ny for k in range(1, ny)]
    barrier = pltpu.get_barrier_semaphore()
    for zz in zpeers:
        pl.semaphore_signal(barrier, inc=1, device_id={"seq": at(zz, y, core)}, device_id_type=MESH)
    for yy in ypeers:
        pl.semaphore_signal(barrier, inc=1, device_id={"seq": at(z, yy, core)}, device_id_type=MESH)
    pl.semaphore_signal(barrier, inc=1, device_id={"seq": at(z, y, 1 - core)}, device_id_type=MESH)

    def rows(ref, owner):
        return ref.at[pl.ds(pl.multiple_of(owner * size, size), size), :]

    locals_ = [
        pltpu.make_async_copy(lat_ref, rows(lat_all, me), lsem.at[0]),
        pltpu.make_async_copy(idx_ref, rows(idx_all, me), lsem.at[1]),
    ]
    for c in locals_:
        c.start()
    pl.semaphore_wait(barrier, nz - 1 + ny - 1 + 1)
    pending = []

    def send(owner, device, ssem, rsem, first):
        src_l = lat_ref if first else rows(lat_all, owner)
        src_i = idx_ref if first else rows(idx_all, owner)
        out = [
            remote(src_l, rows(lat_all, owner), ssem.at[0], rsem.at[0], {"seq": device}),
            remote(src_i, rows(idx_all, owner), ssem.at[1], rsem.at[1], {"seq": device}),
        ]
        for c in out:
            c.start()
        pending.extend(out)

    def receive(owner, sems, rsem):
        remote(lat_ref, rows(lat_all, owner), sems.at[0], rsem.at[0], {"seq": me}).wait_recv()
        remote(idx_ref, rows(idx_all, owner), sems.at[1], rsem.at[1], {"seq": me}).wait_recv()

    for k in range(1, nz):
        send(me, at((z + k) % nz, y, core), zs.at[k], zr.at[k], True)
    for j in range(1, ny):
        send(me, at(z, (y + j) % ny, core), ys.at[0, j], yr.at[0, j], True)
    send(me, at(z, y, 1 - core), cs.at[0, 0], cr.at[0, 0], True)
    for k in range(1, nz):
        owner = at((z - k + nz) % nz, y, core)
        receive(owner, zs.at[k], zr.at[k])
        for j in range(1, ny):
            send(owner, at(z, (y + j) % ny, core), ys.at[k, j], yr.at[k, j], False)
        send(owner, at(z, y, 1 - core), cs.at[k, 0], cr.at[k, 0], False)
    for k in range(nz):
        for j in range(1, ny):
            owner = at((z - k + nz) % nz, (y - j + ny) % ny, core)
            receive(owner, ys.at[k, j], yr.at[k, j])
            send(owner, at(z, y, 1 - core), cs.at[k, j], cr.at[k, j], False)
    for k in range(nz):
        for j in range(ny):
            owner = at((z - k + nz) % nz, (y - j + ny) % ny, 1 - core)
            receive(owner, cs.at[k, j], cr.at[k, j])
    for c in pending:
        c.wait_send()
    for c in locals_:
        c.wait()


def gather_keys(n, latent_keys, index_keys):
    nz, ny = line_sizes(n)
    size, width = latent_keys.shape
    depth = index_keys.shape[1]
    dma = pltpu.SemaphoreType.DMA
    return pl.pallas_call(
        functools.partial(gather_kernel, n),
        out_shape=(
            jax.ShapeDtypeStruct((n * size, width), jnp.bfloat16),
            jax.ShapeDtypeStruct((n * size, depth), jnp.bfloat16),
        ),
        in_specs=[pl.BlockSpec(memory_space=VMEM)] * 2,
        out_specs=(pl.BlockSpec(memory_space=VMEM),) * 2,
        scratch_shapes=[
            dma((2,)),
            dma((nz, 2)), dma((nz, 2)),
            dma((nz, ny, 2)), dma((nz, ny, 2)),
            dma((nz, ny, 2)), dma((nz, ny, 2)),
        ],
        compiler_params=pltpu.CompilerParams(collective_id=0, has_side_effects=True),
        name="gather_keys",
    )(latent_keys, index_keys)


def forward_kernel(sub, vis_ref, lat_ref, idx_ref, w_ref, lk_ref, ik_ref, logit_ref, target_ref):
    row_count, heads, width = lat_ref.shape
    gheads = idx_ref.shape[1]
    key_count = lk_ref.shape[0]
    step = pl.program_id(0)
    ids = lax.broadcasted_iota(jnp.int32, (1, key_count), 1)
    contract = (((1,), (1,)), ((), ()))
    depth_scale = float(idx_ref.shape[2]) ** (-0.5) * INDEX_HEADS ** (-0.5)
    c = mla_scale * LOG2E
    for first in range(0, row_count, sub):
        scores = lax.dot_general(
            lat_ref[first : first + sub].reshape(sub * heads, width), lk_ref[...], contract,
            preferred_element_type=jnp.float32,
        )
        targets = []
        for r in range(sub):
            seen = ids < vis_ref[step * row_count + first + r]
            s = jnp.where(seen, scores[r * heads : (r + 1) * heads], neg_fill)
            peak = jnp.max(s, axis=1, keepdims=True)
            e = jnp.exp2((s - peak) * c)
            scale = (1.0 / MLA_HEADS) / jnp.sum(e, axis=1, keepdims=True)
            targets.append(jnp.sum(e * scale, axis=0, keepdims=True))
        target_ref[first : first + sub, :] = jnp.concatenate(targets, axis=0).astype(target_ref.dtype)
        products = lax.dot_general(
            idx_ref[first : first + sub].reshape(sub * gheads, idx_ref.shape[2]), ik_ref[...], contract,
            preferred_element_type=jnp.float32,
        )
        logits = []
        for r in range(sub):
            p = jnp.maximum(products[r * gheads : (r + 1) * gheads], 0.0)
            w = w_ref[pl.ds((first + r) * gheads, gheads), :] * depth_scale
            logits.append(jnp.sum(p * w, axis=0, keepdims=True))
        logit_ref[first : first + sub, :] = jnp.concatenate(logits, axis=0)


def forward(latent_queries, index_queries, weights, visible, lat_all, idx_all, rows=16, sub=8):
    row_count, heads, width = latent_queries.shape
    gheads, depth = index_queries.shape[1:]
    key_count = lat_all.shape[0]
    grid = (row_count // rows,)
    return pl.pallas_call(
        functools.partial(forward_kernel, sub),
        out_shape=(
            jax.ShapeDtypeStruct((row_count, key_count), jnp.float32),
            jax.ShapeDtypeStruct((row_count, key_count), jnp.float32),
        ),
        grid_spec=pltpu.PrefetchScalarGridSpec(
            num_scalar_prefetch=1,
            grid=grid,
            in_specs=[
                pl.BlockSpec((rows, heads, width), lambda i, v: (i, 0, 0)),
                pl.BlockSpec((rows, gheads, depth), lambda i, v: (i, 0, 0)),
                pl.BlockSpec((rows * gheads, 1), lambda i, v: (i, 0)),
                pl.BlockSpec((key_count, width), lambda i, v: (0, 0)),
                pl.BlockSpec((key_count, depth), lambda i, v: (0, 0)),
            ],
            out_specs=(
                pl.BlockSpec((rows, key_count), lambda i, v: (i, 0)),
                pl.BlockSpec((rows, key_count), lambda i, v: (i, 0)),
            ),
        ),
        name="forward_rows",
    )(visible, latent_queries, index_queries, weights, lat_all, idx_all)


def exchange_kernel(nh, logit_ref, target_ref, vis_ref, slope_ref, logit_got, target_got, target_out, part, got, ss, rs):
    me = lax.axis_index("head")
    share = logit_ref.shape[0] // nh

    def rows_of(owner):
        return pl.ds(pl.multiple_of(owner * share, share), share)

    mine = rows_of(me)
    peers = [(me + k) % nh for k in range(1, nh)]
    sources = [(me - k + nh) % nh for k in range(1, nh)]
    barrier = pltpu.get_barrier_semaphore()
    for peer in peers:
        pl.semaphore_signal(barrier, inc=1, device_id={"head": peer}, device_id_type=MESH)
    target_out[...] = target_ref[...].astype(jnp.bfloat16)
    pl.semaphore_wait(barrier, nh - 1)
    first, second, third = [], [], []
    for k, peer in enumerate(peers):
        first.append(remote(logit_ref.at[rows_of(peer), :], logit_got.at[k], ss.at[0, k], rs.at[0, k], {"head": peer}))
        first[-1].start()
    for k, peer in enumerate(peers):
        second.append(remote(target_out.at[rows_of(peer), :], target_got.at[k], ss.at[1, k], rs.at[1, k], {"head": peer}))
        second[-1].start()
    logits = logit_ref[mine, :]
    for k in range(nh - 1):
        first[k].wait_recv()
        logits = logits + logit_got[k]
    ids = lax.broadcasted_iota(jnp.int32, logits.shape, 1)
    logits = jnp.where(ids < vis_ref[mine, :], logits, neg_fill)
    weights = jnp.exp(logits - jnp.max(logits, axis=1, keepdims=True))
    prob = weights * (1.0 / jnp.sum(weights, axis=1, keepdims=True))
    target = target_ref[mine, :]
    for k in range(nh - 1):
        second[k].wait_recv()
        target = target + target_got[k].astype(jnp.float32)
    slope = loss_weight * (prob - target)
    slope_ref[mine, :] = slope
    part[...] = slope.astype(jnp.bfloat16)
    for k, peer in enumerate(peers):
        third.append(remote(part, got.at[k], ss.at[2, k], rs.at[2, k], {"head": peer}))
        third[-1].start()
    for k, source in enumerate(sources):
        third[k].wait_recv()
        slope_ref[rows_of(source), :] = got[k].astype(jnp.float32)
    for copy in first + second + third:
        copy.wait_send()


def exchange(nh, logits, targets, visible):
    row_count, key_count = logits.shape
    share = row_count // nh
    dma = pltpu.SemaphoreType.DMA
    return pl.pallas_call(
        functools.partial(exchange_kernel, nh),
        out_shape=jax.ShapeDtypeStruct((row_count, key_count), jnp.float32),
        in_specs=[pl.BlockSpec(memory_space=VMEM)] * 3,
        out_specs=pl.BlockSpec(memory_space=VMEM),
        scratch_shapes=[
            VMEM((nh - 1, share, key_count), jnp.float32),
            VMEM((nh - 1, share, key_count), jnp.bfloat16),
            VMEM((row_count, key_count), jnp.bfloat16),
            VMEM((share, key_count), jnp.bfloat16),
            VMEM((nh - 1, share, key_count), jnp.bfloat16),
            dma((3, nh - 1)), dma((3, nh - 1)),
        ],
        compiler_params=pltpu.CompilerParams(collective_id=1, has_side_effects=True),
        name="head_exchange",
    )(logits, targets, visible)


def backward_kernel(idx_ref, w_ref, ik_ref, slope_ref, qgrad_ref, wgrad_ref, kgrad_ref, total):
    rows, gheads, depth = idx_ref.shape
    dot_scale = float(depth) ** (-0.5)
    head_scale = INDEX_HEADS ** (-0.5)
    step = pl.program_id(0)

    @pl.when(step == 0)
    def _():
        total[...] = jnp.zeros_like(total)

    queries = idx_ref[...].reshape(rows * gheads, depth)
    products = lax.dot_general(
        queries, ik_ref[...], (((1,), (1,)), ((), ())), preferred_element_type=jnp.float32
    )
    edges = []
    sums = []
    for r in range(rows):
        p = products[r * gheads : (r + 1) * gheads]
        slope = slope_ref[r : r + 1, :]
        w = w_ref[r * gheads : (r + 1) * gheads, :] * head_scale
        edges.append(jnp.where(p > 0.0, slope * w, 0.0).astype(jnp.bfloat16))
        sums.append(jnp.sum(slope * jnp.maximum(p, 0.0), axis=1, keepdims=True))
    edge = jnp.concatenate(edges, axis=0)
    wgrad_ref[...] = jnp.concatenate(sums, axis=0) * (head_scale * dot_scale)
    qgrad = jnp.dot(edge, ik_ref[...], preferred_element_type=jnp.float32) * dot_scale
    qgrad_ref[...] = qgrad.astype(jnp.bfloat16).reshape(rows, gheads, depth)
    total[...] += lax.dot_general(
        queries, edge, (((0,), (0,)), ((), ())), preferred_element_type=jnp.float32
    )

    @pl.when(step == pl.num_programs(0) - 1)
    def _():
        kgrad_ref[...] = (total[...] * dot_scale).T.astype(jnp.bfloat16)


def backward(index_queries, weights, idx_all, slope, rows=16):
    row_count, gheads, depth = index_queries.shape
    key_count = idx_all.shape[0]
    return pl.pallas_call(
        backward_kernel,
        out_shape=(
            jax.ShapeDtypeStruct((row_count, gheads, depth), jnp.bfloat16),
            jax.ShapeDtypeStruct((row_count * gheads, 1), jnp.float32),
            jax.ShapeDtypeStruct((key_count, depth), jnp.bfloat16),
        ),
        grid=(row_count // rows,),
        in_specs=[
            pl.BlockSpec((rows, gheads, depth), lambda i: (i, 0, 0)),
            pl.BlockSpec((rows * gheads, 1), lambda i: (i, 0)),
            pl.BlockSpec((key_count, depth), lambda i: (0, 0)),
            pl.BlockSpec((rows, key_count), lambda i: (i, 0)),
        ],
        out_specs=(
            pl.BlockSpec((rows, gheads, depth), lambda i: (i, 0, 0)),
            pl.BlockSpec((rows * gheads, 1), lambda i: (i, 0)),
            pl.BlockSpec((key_count, depth), lambda i: (0, 0)),
        ),
        scratch_shapes=[VMEM((depth, key_count), jnp.float32)],
        name="index_backward",
    )(index_queries, weights, idx_all, slope)


def owner_kernel(n, nh, term_ref, out_ref, got, mine, peer, ss, rs, hs, hr):
    me = lax.axis_index("seq")
    head = lax.axis_index("head")
    size = out_ref.shape[0]
    barrier = pltpu.get_barrier_semaphore()
    for k in range(1, n):
        pl.semaphore_signal(barrier, inc=1, device_id={"seq": (me + k) % n}, device_id_type=MESH)
    for k in range(1, nh):
        pl.semaphore_signal(barrier, inc=1, device_id={"head": (head + k) % nh}, device_id_type=MESH)
    pl.semaphore_wait(barrier, n - 1 + nh - 1)
    copies = []
    for k in range(1, n):
        to = (me + k) % n
        copy = remote(
            term_ref.at[pl.ds(pl.multiple_of(to * size, size), size), :],
            got.at[k - 1], ss.at[k - 1], rs.at[k - 1], {"seq": to},
        )
        copy.start()
        copies.append(copy)
    total = term_ref[pl.ds(pl.multiple_of(me * size, size), size), :].astype(jnp.float32)
    for k in range(n - 1):
        copies[k].wait_recv()
        total = total + got[k].astype(jnp.float32)
    mine[...] = total
    last = []
    for k in range(1, nh):
        last.append(remote(mine, peer.at[k - 1], hs.at[k - 1], hr.at[k - 1], {"head": (head + k) % nh}))
        last[-1].start()
    for copy in copies:
        copy.wait_send()
    for k in range(nh - 1):
        last[k].wait_recv()
        total = total + peer[k]
    for copy in last:
        copy.wait_send()
    out_ref[...] = total


def owner_sum(n, nh, term):
    key_count, depth = term.shape
    size = key_count // n
    dma = pltpu.SemaphoreType.DMA
    return pl.pallas_call(
        functools.partial(owner_kernel, n, nh),
        out_shape=jax.ShapeDtypeStruct((size, depth), jnp.float32),
        in_specs=[pl.BlockSpec(memory_space=VMEM)],
        out_specs=pl.BlockSpec(memory_space=VMEM),
        scratch_shapes=[
            VMEM((n - 1, size, depth), jnp.bfloat16),
            VMEM((size, depth), jnp.float32),
            VMEM((nh - 1, size, depth), jnp.float32),
            dma((n - 1,)), dma((n - 1,)), dma((nh - 1,)), dma((nh - 1,)),
        ],
        compiler_params=pltpu.CompilerParams(collective_id=2, has_side_effects=True),
        name="owner_sum",
    )(term)


def body(n, nh, latent_queries, latent_keys, index_queries, index_keys, head_weights, visible):
    row_count, gheads = head_weights.shape
    weights = head_weights.reshape(row_count * gheads, 1)
    lat_all, idx_all = gather_keys(n, latent_keys, index_keys)
    logits, targets = forward(latent_queries, index_queries, weights, visible, lat_all, idx_all)
    slope = exchange(nh, logits, targets, visible.reshape(row_count, 1))
    query_grad, weight_grad, term = backward(index_queries, weights, idx_all, slope)
    key_grad = owner_sum(n, nh, term)
    return query_grad, weight_grad.reshape(row_count, gheads), key_grad


def solution(mesh):
    placed = (
        P("seq", "head", None),
        P("seq", None),
        P("seq", "head", None),
        P("seq", None),
        P("seq", "head"),
        P("seq"),
    )
    return jax.shard_map(
        functools.partial(body, mesh.shape["seq"], mesh.shape["head"]),
        mesh=mesh,
        in_specs=placed,
        out_specs=(P("seq", "head", None), P("seq", "head"), P("seq", None)),
        check_vma=False,
    )
```

time: 282 us -> 119 us (0.42)
  Pallas kernels: 0 us -> 93.2 us
  waiting for transfers between devices: 52.6 us -> 0 us
  matrix products: 52.3 us -> 0 us
  blocking collectives: 52.1 us -> 0 us
  other arithmetic: 51.1 us -> 2.2 us
  local copies, waits for them, and re-layouts: 55.9 us -> 22 us
  between operations: 15.6 us -> 0.67 us
    pallas_call x0 -> x5, Pallas kernels: none -> 93.2 us  [the longest x1 28.8 us: forward(): pl.pallas_call(functools.partial(forward_kernel, sub), out_shape=(jax.Sha...]
    dot_general x9 -> x0, matrix products: 52.3 us -> none  [the longest x1 23.2 us: latent_scores(): lax.dot_general(portion, flat, (((1,), (1,)), ((), ())), preferred_elemen...]
    reduce_scatter x3 -> x0, waiting for transfers between devices: 51.8 us -> none  [the longest x1 51.8 us: body(): owned = lax.psum_scatter(key_term, 'seq', scatter_dimension=0, tiled=True)]
    exp x1 -> x0, local copies, waits for them, and re-layouts: 33.4 us -> none  [target_update(): probs = jnp.exp(scores - normalizer.reshape(1, row_count * head_count))]
    all_gather x2 -> x0, blocking collectives: 32.7 us -> none  [the longest x1 24.2 us: body(): collected = lax.all_gather(index_keys, 'seq', axis=0, tiled=True)]
    reduce_sum x3 -> x0, other arithmetic: 30 us -> none  [the longest x1 15.8 us: stats_update(): new_total = jnp.sum(jnp.exp(scores - new_max[None, :]), axis=0)]
    psum x2 -> x0, blocking collectives: 14.5 us -> none  [the longest x1 9.55 us: body(): key_grad = lax.psum(owned, 'head')]
    exp x1 -> x0, other arithmetic: 12.5 us -> none  [target_update(): probs = jnp.exp(scores - normalizer.reshape(1, row_count * head_count))]
  transfers between devices with their start and end apart: 4 -> 0, of which waited for: 1 -> 0; matrix products, arithmetic and copies ran while one was open for 45% -> 0% of each run, Pallas kernels for 0% -> 0%
where the time goes in v1:
time: 119 us; the launch traced here: 118 us
  Pallas kernels  93.2 us (78%)
  local copies, waits for them, and re-layouts  22 us (18%)
  other arithmetic  2.2 us (2%)
    pallas_call x1, Pallas kernels, forward(): pl.pallas_call(functools.partial(forward_kernel, sub), out_shape=(jax.Sha...  28.8 us
    pallas_call x1, Pallas kernels, gather_keys(): pl.pallas_call(functools.partial(gather_kernel, n), out_shape=(jax.ShapeD...  22.4 us
    pallas_call x1, Pallas kernels, exchange(): pl.pallas_call(functools.partial(exchange_kernel, nh), out_shape=jax.Shap...  18.2 us
    unnamed x6, local copies, waits for them, and re-layouts  17.7 us
    pallas_call x1, Pallas kernels, owner_sum(): pl.pallas_call(functools.partial(owner_kernel, n, nh), out_shape=jax.Shap...  13.5 us
    pallas_call x1, Pallas kernels, backward(): pl.pallas_call(backward_kernel, out_shape=(jax.ShapeDtypeStruct((row_coun...  10.4 us
    reshape x1, local copies, waits for them, and re-layouts, body(): weights = head_weights.reshape(row_count * gheads, 1)  3.47 us

profile of v1, /device:TPU:0, one launch (start us, length us, event | category | flops | bytes accessed | tf_op | source)
XLA Modules:
  0.0 118.1 jit_solution(11427777974057365934)
XLA Ops:
  0.6 22.4 %gather_keys.1 = (bf16[1024,576]{1,0:T(8,128)(2,1)}, bf16[1024,128]{1,0:T(8,128)(2,1)}) custom-call(bf16[64,576]{1,0:T(8,128)(2,1)} %lat_ref.2, bf16[64,128]{1,0:T(8,128)(2,1)} %idx_ref.3), custom_call_target="tpu_custom_call" | custom-call | tf_op jit(solution)/shard_map/gather_keys/pallas_call | solution.py:109
  23.0 0.8 copy.13
  23.8 3.5 %reshape.18.w_ref = f32[4096,1]{1,0:T(8,128)} reshape(f32[128,32]{1,0:T(8,128)S(1)} %copy.13) | data formatting | bytes 32768 | tf_op jit(solution)/shard_map/reshape | solution.py:384
  27.3 14.8 %copy.14.lat_ref = bf16[128,64,576]{2,1,0:T(8,128)(2,1)} copy(bf16[128,64,576]{0,2,1:T(8,128)(2,1)} %param.6) | data formatting | bytes 18874368 | tf_op args[0]
  42.1 0.0 copy-start
  42.1 28.8 %forward_rows.1 = (f32[128,1024]{1,0:T(8,128)}, f32[128,1024]{1,0:T(8,128)}) custom-call(s32[128]{0:T(128)} %vis_ref.1, bf16[128,64,576]{2,1,0:T(8,128)(2,1)} %copy.14.lat_ref, bf16[128,32,128]{2,1,0:T(8,128)(2,1)} %idx_ref.5, f32[4096,1]{1,0:T(8,128)} %reshape.18.w_ref, bf16[1024,576]{1,0:T(8,128)(2,1)} %get-tuple-element.11.lk_ref, ...), custom_call_target="tpu_custom_call" | custom-call | tf_op jit(solution)/shard_map/forward_rows/pallas_call | solution.py:168
  70.9 0.0 copy-done
  70.9 0.7 copy.16.vis_ref
  71.6 18.2 %head_exchange.1.slope_ref = f32[128,1024]{1,0:T(8,128)} custom-call(f32[128,1024]{1,0:T(8,128)} %get-tuple-element.12.logit_ref, f32[128,1024]{1,0:T(8,128)} %get-tuple-element.13.target_ref, s32[128,1]{1,0:T(8,128)} %copy.16.vis_ref), custom_call_target="tpu_custom_call" | custom-call | tf_op jit(solution)/shard_map/head_exchange/pallas_call | solution.py:244
  89.9 10.4 %index_backward.1 = (bf16[128,32,128]{2,1,0:T(8,128)(2,1)}, f32[4096,1]{1,0:T(8,128)}, bf16[1024,128]{1,0:T(8,128)(2,1)}) custom-call(bf16[128,32,128]{2,1,0:T(8,128)(2,1)} %idx_ref.5, f32[4096,1]{1,0:T(8,128)} %reshape.18.w_ref, bf16[1024,128]{1,0:T(8,128)(2,1)} %get-tuple-element.10.ik_ref, f32[128,1024]{1,0:T(8,128)} %head_exchange.1.slope_ref), custom_call_target="tpu_custom_call" | custom-call | tf_op jit(solution)/shard_map/index_backward/pallas_call | solution.py:300
  100.2 2.2 %reduce = f32[4096]{0:T(1024)S(1)} reduce(f32[4096,1]{1,0:T(8,128)} %get-tuple-element.15, f32[]{:T(128)} %constant), dimensions={1}, to_apply=%get-tuple-element.15.reduce_sub_computation | reduce | bytes 32772 | tf_op jit(solution)/shard_map/index_backward/pallas_call | solution.py:300
  102.4 0.1 reshape.17
  102.5 0.7 copy.18
  103.2 13.5 %owner_sum.1 = f32[64,128]{1,0:T(8,128)} custom-call(bf16[1024,128]{1,0:T(8,128)(2,1)} %get-tuple-element.16.term_ref), custom_call_target="tpu_custom_call" | custom-call | tf_op jit(solution)/shard_map/owner_sum/pallas_call | solution.py:366
  116.7 1.4 %copy.20 = f32[64,128]{1,0:T(8,128)} copy(f32[64,128]{1,0:T(8,128)} %owner_sum.1) | data formatting | bytes 65536
Async XLA Ops:
  42.1 28.8 %copy-start = (s32[128]{0:T(128)S(1)}, s32[128]{0:T(128)}, u32[]{:S(2)}) copy-start(s32[128]{0:T(128)} %vis_ref.1) | copy-start | bytes 1540

commit v2 on v1

--- a/solution.py
+++ b/solution.py
@@ -125,69 +125,99 @@
     )(latent_keys, index_keys)
 
 
-def forward_kernel(sub, vis_ref, lat_ref, idx_ref, w_ref, lk_ref, ik_ref, logit_ref, target_ref):
-    row_count, heads, width = lat_ref.shape
-    gheads = idx_ref.shape[1]
+def forward_kernel(
+    vis_ref, lat_ref, idx_ref, w_ref, lk_ref, ik_ref, logit_ref, target_ref, split_ref, wide, bias, total
+):
+    block, width, row_count = lat_ref.shape
+    gheads = w_ref.shape[0]
     key_count = lk_ref.shape[0]
+    depth = ik_ref.shape[1]
     step = pl.program_id(0)
-    ids = lax.broadcasted_iota(jnp.int32, (1, key_count), 1)
-    contract = (((1,), (1,)), ((), ()))
-    depth_scale = float(idx_ref.shape[2]) ** (-0.5) * INDEX_HEADS ** (-0.5)
     c = mla_scale * LOG2E
-    for first in range(0, row_count, sub):
-        scores = lax.dot_general(
-            lat_ref[first : first + sub].reshape(sub * heads, width), lk_ref[...], contract,
-            preferred_element_type=jnp.float32,
-        )
-        targets = []
-        for r in range(sub):
-            seen = ids < vis_ref[step * row_count + first + r]
-            s = jnp.where(seen, scores[r * heads : (r + 1) * heads], neg_fill)
-            peak = jnp.max(s, axis=1, keepdims=True)
+
+    @pl.when(step == 0)
+    def _():
+        ids = lax.broadcasted_iota(jnp.int32, (key_count, row_count), 0)
+        bias[...] = jnp.where(ids < vis_ref[...], 0.0, neg_fill)
+        wide[...] = idx_ref[...].astype(jnp.float32)
+        total[...] = jnp.zeros_like(total)
+        scale = float(depth) ** (-0.5) * INDEX_HEADS ** (-0.5)
+
+        def pair(number, _):
+            g = number * 2
+            parts = [wide[pl.ds(g + j, row_count, stride=gheads), :].astype(jnp.bfloat16) for j in range(2)]
+            for j in range(2):
+                split_ref[g + j] = parts[j]
+            products = lax.dot_general(
+                ik_ref[...], jnp.concatenate(parts, axis=0), (((1,), (1,)), ((), ())),
+                preferred_element_type=jnp.float32,
+            )
+            w = w_ref[pl.ds(g, 2), :] * scale
+            total[...] += (
+                jnp.maximum(products[:, :row_count], 0.0) * w[0:1]
+                + jnp.maximum(products[:, row_count:], 0.0) * w[1:2]
+            )
+            return 0
+
+        lax.fori_loop(0, gheads // 2, pair, 0)
+        logit_ref[...] = total[...].T
+        total[...] = jnp.zeros_like(total)
+
+    def scores_of(j):
+        queries = jnp.concatenate([lat_ref[2 * j], lat_ref[2 * j + 1]], axis=1)
+        return jnp.dot(lk_ref[...], queries, preferred_element_type=jnp.float32)
+
+    scores = scores_of(0)
+    for j in range(block // 2):
+        following = scores_of(j + 1) if j + 1 < block // 2 else None
+        added = None
+        for part in range(2):
+            s = scores[:, part * row_count : (part + 1) * row_count] + bias[...]
+            peak = jnp.max(s, axis=0, keepdims=True)
             e = jnp.exp2((s - peak) * c)
-            scale = (1.0 / MLA_HEADS) / jnp.sum(e, axis=1, keepdims=True)
-            targets.append(jnp.sum(e * scale, axis=0, keepdims=True))
-        target_ref[first : first + sub, :] = jnp.concatenate(targets, axis=0).astype(target_ref.dtype)
-        products = lax.dot_general(
-            idx_ref[first : first + sub].reshape(sub * gheads, idx_ref.shape[2]), ik_ref[...], contract,
-            preferred_element_type=jnp.float32,
-        )
-        logits = []
-        for r in range(sub):
-            p = jnp.maximum(products[r * gheads : (r + 1) * gheads], 0.0)
-            w = w_ref[pl.ds((first + r) * gheads, gheads), :] * depth_scale
-            logits.append(jnp.sum(p * w, axis=0, keepdims=True))
-        logit_ref[first : first + sub, :] = jnp.concatenate(logits, axis=0)
-
-
-def forward(latent_queries, index_queries, weights, visible, lat_all, idx_all, rows=16, sub=8):
-    row_count, heads, width = latent_queries.shape
-    gheads, depth = index_queries.shape[1:]
-    key_count = lat_all.shape[0]
-    grid = (row_count // rows,)
+            term = e * ((1.0 / MLA_HEADS) / jnp.sum(e, axis=0, keepdims=True))
+            added = term if added is None else added + term
+        total[...] += added
+        scores = following
+
+    @pl.when(step == pl.num_programs(0) - 1)
+    def _():
+        target_ref[...] = total[...].T
+
+
+def forward(latent_t, index_flat, weights_t, visible, lat_all, idx_all, block=8):
+    heads, width, row_count = latent_t.shape
+    gheads = weights_t.shape[0]
+    key_count, depth = idx_all.shape
+    whole = lambda *shape: pl.BlockSpec(shape, lambda i: (0,) * len(shape))
     return pl.pallas_call(
-        functools.partial(forward_kernel, sub),
+        forward_kernel,
         out_shape=(
             jax.ShapeDtypeStruct((row_count, key_count), jnp.float32),
             jax.ShapeDtypeStruct((row_count, key_count), jnp.float32),
+            jax.ShapeDtypeStruct((gheads, row_count, depth), jnp.bfloat16),
         ),
-        grid_spec=pltpu.PrefetchScalarGridSpec(
-            num_scalar_prefetch=1,
-            grid=grid,
-            in_specs=[
-                pl.BlockSpec((rows, heads, width), lambda i, v: (i, 0, 0)),
-                pl.BlockSpec((rows, gheads, depth), lambda i, v: (i, 0, 0)),
-                pl.BlockSpec((rows * gheads, 1), lambda i, v: (i, 0)),
-                pl.BlockSpec((key_count, width), lambda i, v: (0, 0)),
-                pl.BlockSpec((key_count, depth), lambda i, v: (0, 0)),
-            ],
-            out_specs=(
-                pl.BlockSpec((rows, key_count), lambda i, v: (i, 0)),
-                pl.BlockSpec((rows, key_count), lambda i, v: (i, 0)),
-            ),
+        grid=(heads // block,),
+        in_specs=[
+            whole(1, row_count),
+            pl.BlockSpec((block, width, row_count), lambda i: (i, 0, 0)),
+            whole(row_count * gheads, depth),
+            whole(gheads, row_count),
+            whole(key_count, width),
+            whole(key_count, depth),
+        ],
+        out_specs=(
+            whole(row_count, key_count),
+            whole(row_count, key_count),
+            whole(gheads, row_count, depth),
         ),
+        scratch_shapes=[
+            VMEM((row_count * gheads, depth), jnp.float32),
+            VMEM((key_count, row_count), jnp.float32),
+            VMEM((key_count, row_count), jnp.float32),
+        ],
         name="forward_rows",
-    )(visible, latent_queries, index_queries, weights, lat_all, idx_all)
+    )(visible, latent_t, index_flat, weights_t, lat_all, idx_all)
 
 
 def exchange_kernel(nh, logit_ref, target_ref, vis_ref, slope_ref, logit_got, target_got, target_out, part, got, ss, rs):
@@ -259,8 +289,9 @@
     )(logits, targets, visible)
 
 
-def backward_kernel(idx_ref, w_ref, ik_ref, slope_ref, qgrad_ref, wgrad_ref, kgrad_ref, total):
-    rows, gheads, depth = idx_ref.shape
+def backward_kernel(split_ref, w_ref, ik_ref, slope_ref, qgrad_ref, wgrad_ref, kgrad_ref, slope, ikt, total, wide):
+    block, row_count, depth = split_ref.shape
+    gheads = wide.shape[0] // row_count
     dot_scale = float(depth) ** (-0.5)
     head_scale = INDEX_HEADS ** (-0.5)
     step = pl.program_id(0)
@@ -268,57 +299,68 @@
     @pl.when(step == 0)
     def _():
         total[...] = jnp.zeros_like(total)
-
-    queries = idx_ref[...].reshape(rows * gheads, depth)
-    products = lax.dot_general(
-        queries, ik_ref[...], (((1,), (1,)), ((), ())), preferred_element_type=jnp.float32
-    )
-    edges = []
+        slope[...] = slope_ref[...].T
+        ikt[...] = ik_ref[...].astype(jnp.float32).T.astype(jnp.bfloat16)
+
+    w = w_ref[...] * head_scale
     sums = []
-    for r in range(rows):
-        p = products[r * gheads : (r + 1) * gheads]
-        slope = slope_ref[r : r + 1, :]
-        w = w_ref[r * gheads : (r + 1) * gheads, :] * head_scale
-        edges.append(jnp.where(p > 0.0, slope * w, 0.0).astype(jnp.bfloat16))
-        sums.append(jnp.sum(slope * jnp.maximum(p, 0.0), axis=1, keepdims=True))
-    edge = jnp.concatenate(edges, axis=0)
+    for j in range(block // 2):
+        queries = split_ref[2 * j : 2 * j + 2].reshape(2 * row_count, depth)
+        products = lax.dot_general(
+            ik_ref[...], queries, (((1,), (1,)), ((), ())), preferred_element_type=jnp.float32
+        )
+        edges = []
+        for part in range(2):
+            p = products[:, part * row_count : (part + 1) * row_count]
+            g = 2 * j + part
+            edges.append(jnp.where(p > 0.0, slope[...] * w[g : g + 1], 0.0).astype(jnp.bfloat16))
+            sums.append(jnp.sum(slope[...] * jnp.maximum(p, 0.0), axis=0, keepdims=True))
+        edge = jnp.concatenate(edges, axis=1)
+        total[...] += jnp.dot(edge, queries, preferred_element_type=jnp.float32)
+        qgrad = (jnp.dot(ikt[...], edge, preferred_element_type=jnp.float32) * dot_scale).T
+        for part in range(2):
+            wide[pl.ds(step * block + 2 * j + part, row_count, stride=gheads), :] = qgrad[
+                part * row_count : (part + 1) * row_count
+            ]
     wgrad_ref[...] = jnp.concatenate(sums, axis=0) * (head_scale * dot_scale)
-    qgrad = jnp.dot(edge, ik_ref[...], preferred_element_type=jnp.float32) * dot_scale
-    qgrad_ref[...] = qgrad.astype(jnp.bfloat16).reshape(rows, gheads, depth)
-    total[...] += lax.dot_general(
-        queries, edge, (((0,), (0,)), ((), ())), preferred_element_type=jnp.float32
-    )
 
     @pl.when(step == pl.num_programs(0) - 1)
     def _():
-        kgrad_ref[...] = (total[...] * dot_scale).T.astype(jnp.bfloat16)
-
-
-def backward(index_queries, weights, idx_all, slope, rows=16):
-    row_count, gheads, depth = index_queries.shape
+        kgrad_ref[...] = (total[...] * dot_scale).astype(jnp.bfloat16)
+        qgrad_ref[...] = wide[...].astype(jnp.bfloat16)
+
+
+def backward(split, weights_t, idx_all, slope, block=8):
+    gheads, row_count, depth = split.shape
     key_count = idx_all.shape[0]
+    whole = lambda *shape: pl.BlockSpec(shape, lambda i: (0,) * len(shape))
     return pl.pallas_call(
         backward_kernel,
         out_shape=(
-            jax.ShapeDtypeStruct((row_count, gheads, depth), jnp.bfloat16),
-            jax.ShapeDtypeStruct((row_count * gheads, 1), jnp.float32),
+            jax.ShapeDtypeStruct((row_count * gheads, depth), jnp.bfloat16),
+            jax.ShapeDtypeStruct((gheads, row_count), jnp.float32),
             jax.ShapeDtypeStruct((key_count, depth), jnp.bfloat16),
         ),
-        grid=(row_count // rows,),
+        grid=(gheads // block,),
         in_specs=[
-            pl.BlockSpec((rows, gheads, depth), lambda i: (i, 0, 0)),
-            pl.BlockSpec((rows * gheads, 1), lambda i: (i, 0)),
-            pl.BlockSpec((key_count, depth), lambda i: (0, 0)),
-            pl.BlockSpec((rows, key_count), lambda i: (i, 0)),
+            pl.BlockSpec((block, row_count, depth), lambda i: (i, 0, 0)),
+            pl.BlockSpec((block, row_count), lambda i: (i, 0)),
+            whole(key_count, depth),
+            whole(row_count, key_count),
         ],
         out_specs=(
-            pl.BlockSpec((rows, gheads, depth), lambda i: (i, 0, 0)),
-            pl.BlockSpec((rows * gheads, 1), lambda i: (i, 0)),
-            pl.BlockSpec((key_count, depth), lambda i: (0, 0)),
+            whole(row_count * gheads, depth),
+            pl.BlockSpec((block, row_count), lambda i: (i, 0)),
+            whole(key_count, depth),
         ),
-        scratch_shapes=[VMEM((depth, key_count), jnp.float32)],
+        scratch_shapes=[
+            VMEM((key_count, row_count), jnp.float32),
+            VMEM((depth, key_count), jnp.bfloat16),
+            VMEM((key_count, depth), jnp.float32),
+            VMEM((row_count * gheads, depth), jnp.float32),
+        ],
         name="index_backward",
-    )(index_queries, weights, idx_all, slope)
+    )(split, weights_t, idx_all, slope)
 
 
 def owner_kernel(n, nh, term_ref, out_ref, got, mine, peer, ss, rs, hs, hr):
@@ -380,14 +422,21 @@
 
 
 def body(n, nh, latent_queries, latent_keys, index_queries, index_keys, head_weights, visible):
-    row_count, gheads = head_weights.shape
-    weights = head_weights.reshape(row_count * gheads, 1)
+    row_count, gheads, depth = index_queries.shape
+    weights_t = head_weights.T
     lat_all, idx_all = gather_keys(n, latent_keys, index_keys)
-    logits, targets = forward(latent_queries, index_queries, weights, visible, lat_all, idx_all)
+    logits, targets, split = forward(
+        jnp.transpose(latent_queries, (1, 2, 0)),
+        index_queries.reshape(row_count * gheads, depth),
+        weights_t,
+        visible.reshape(1, row_count),
+        lat_all,
+        idx_all,
+    )
     slope = exchange(nh, logits, targets, visible.reshape(row_count, 1))
-    query_grad, weight_grad, term = backward(index_queries, weights, idx_all, slope)
+    query_grad, weight_grad, term = backward(split, weights_t, idx_all, slope)
     key_grad = owner_sum(n, nh, term)
-    return query_grad, weight_grad.reshape(row_count, gheads), key_grad
+    return query_grad.reshape(row_count, gheads, depth), weight_grad.T, key_grad
 
 
 def solution(mesh):

time: 119 us -> 102 us (0.86)
  local copies, waits for them, and re-layouts: 22 us -> 2.11 us
  Pallas kernels: 93.2 us -> 99 us
  other arithmetic: 2.2 us -> 0 us
    unnamed x6 -> x3, local copies, waits for them, and re-layouts: 17.7 us -> 1.38 us
    pallas_call x1, Pallas kernels: 28.8 us -> 33.7 us  [forward(): pl.pallas_call(forward_kernel, out_shape=(jax.ShapeDtypeStruct((row_count...]
    reshape x2 -> x0, local copies, waits for them, and re-layouts: 3.54 us -> none  [the longest x1 3.47 us: body(): weights = head_weights.reshape(row_count * gheads, 1)]
    pallas_call x1 -> x0, other arithmetic: 2.2 us -> none  [backward(): pl.pallas_call(backward_kernel, out_shape=(jax.ShapeDtypeStruct((row_coun...]
where the time goes in v2:
time: 102 us
  Pallas kernels  99 us (97%)
  local copies, waits for them, and re-layouts  2.11 us (2%)
    pallas_call x1, Pallas kernels, forward(): pl.pallas_call(forward_kernel, out_shape=(jax.ShapeDtypeStruct((row_count...  33.7 us
    pallas_call x1, Pallas kernels, gather_keys(): pl.pallas_call(functools.partial(gather_kernel, n), out_shape=(jax.ShapeD...  22.3 us
    pallas_call x1, Pallas kernels, exchange(): pl.pallas_call(functools.partial(exchange_kernel, nh), out_shape=jax.Shap...  18.3 us
    pallas_call x1, Pallas kernels, owner_sum(): pl.pallas_call(functools.partial(owner_kernel, n, nh), out_shape=jax.Shap...  13.4 us
    pallas_call x1, Pallas kernels, backward(): pl.pallas_call(backward_kernel, out_shape=(jax.ShapeDtypeStruct((row_coun...  11.3 us

profile of v2, /device:TPU:0, one launch (start us, length us, event | category | flops | bytes accessed | tf_op | source)
XLA Modules:
  0.0 101.8 jit_solution(17982958891417350501)
XLA Ops:
  0.6 0.0 copy-start
  0.6 22.3 %gather_keys.1 = (bf16[1024,576]{1,0:T(8,128)(2,1)}, bf16[1024,128]{1,0:T(8,128)(2,1)}) custom-call(bf16[64,576]{1,0:T(8,128)(2,1)} %lat_ref.1, bf16[64,128]{1,0:T(8,128)(2,1)} %idx_ref.1), custom_call_target="tpu_custom_call" | custom-call | tf_op jit(solution)/shard_map/gather_keys/pallas_call | solution.py:109
  23.0 33.7 %forward_rows.1 = (f32[128,1024]{1,0:T(8,128)}, f32[128,1024]{1,0:T(8,128)}, bf16[32,128,128]{2,1,0:T(8,128)(2,1)}) custom-call(s32[1,128]{1,0:T(1,128)} %bitcast.11, bf16[64,576,128]{2,1,0:T(8,128)(2,1)} %bitcast.7, bf16[4096,128]{1,0:T(8,128)(2,1)} %bitcast.8, f32[32,128]{1,0:T(8,128)} %bitcast.9, bf16[1024,576]{1,0:T(8,128)(2,1)} %get-tuple-element.11.lk_ref, ...), custom_call_target="tpu_custom_call" | custom-call | tf_op jit(solution)/shard_map/forward_rows/pallas_call | solution.py:193
  56.7 0.0 copy-done
  56.7 0.7 copy.9.vis_ref
  57.4 18.3 %head_exchange.1.slope_ref = f32[128,1024]{1,0:T(8,128)} custom-call(f32[128,1024]{1,0:T(8,128)} %get-tuple-element.14.logit_ref, f32[128,1024]{1,0:T(8,128)} %get-tuple-element.15.target_ref, s32[128,1]{1,0:T(8,128)} %copy.9.vis_ref), custom_call_target="tpu_custom_call" | custom-call | tf_op jit(solution)/shard_map/head_exchange/pallas_call | solution.py:274
  75.7 11.3 %index_backward.1 = (bf16[4096,128]{1,0:T(8,128)(2,1)}, f32[32,128]{1,0:T(8,128)}, bf16[1024,128]{1,0:T(8,128)(2,1)}) custom-call(bf16[32,128,128]{2,1,0:T(8,128)(2,1)} %get-tuple-element.13.split_ref, f32[32,128]{1,0:T(8,128)} %bitcast.10, bf16[1024,128]{1,0:T(8,128)(2,1)} %get-tuple-element.12.ik_ref, f32[128,1024]{1,0:T(8,128)} %head_exchange.1.slope_ref), custom_call_target="tpu_custom_call" | custom-call | tf_op jit(solution)/shard_map/index_backward/pallas_call | solution.py:337
  87.0 13.4 %owner_sum.1 = f32[64,128]{1,0:T(8,128)} custom-call(bf16[1024,128]{1,0:T(8,128)(2,1)} %get-tuple-element.18.term_ref), custom_call_target="tpu_custom_call" | custom-call | tf_op jit(solution)/shard_map/owner_sum/pallas_call | solution.py:408
  100.4 1.4 %copy.11 = f32[64,128]{1,0:T(8,128)} copy(f32[64,128]{1,0:T(8,128)} %owner_sum.1) | data formatting | bytes 65536
Async XLA Ops:
  0.6 56.0 %copy-start = (s32[128]{0:T(128)S(1)}, s32[128]{0:T(128)}, u32[]{:S(2)}) copy-start(s32[128]{0:T(128)} %param.11) | copy-start | bytes 1540

commit v3 on v2

--- a/solution.py
+++ b/solution.py
@@ -125,13 +125,55 @@
     )(latent_keys, index_keys)
 
 
-def forward_kernel(
-    vis_ref, lat_ref, idx_ref, w_ref, lk_ref, ik_ref, logit_ref, target_ref, split_ref, wide, bias, total
-):
+def logits_kernel(idx_ref, w_ref, ik_ref, logit_ref, split_ref, wide, total):
+    gheads, row_count = w_ref.shape
+    depth = ik_ref.shape[1]
+    wide[...] = idx_ref[...].astype(jnp.float32)
+    total[...] = jnp.zeros_like(total)
+    scale = float(depth) ** (-0.5) * INDEX_HEADS ** (-0.5)
+
+    def pair(number, _):
+        g = number * 2
+        parts = [wide[pl.ds(g + j, row_count, stride=gheads), :].astype(jnp.bfloat16) for j in range(2)]
+        for j in range(2):
+            split_ref[g + j] = parts[j]
+        products = lax.dot_general(
+            ik_ref[...], jnp.concatenate(parts, axis=0), (((1,), (1,)), ((), ())),
+            preferred_element_type=jnp.float32,
+        )
+        w = w_ref[pl.ds(g, 2), :] * scale
+        total[...] += (
+            jnp.maximum(products[:, :row_count], 0.0) * w[0:1]
+            + jnp.maximum(products[:, row_count:], 0.0) * w[1:2]
+        )
+        return 0
+
+    lax.fori_loop(0, gheads // 2, pair, 0)
+    logit_ref[...] = total[...].T
+
+
+def index_forward(index_flat, weights_t, idx_all):
+    gheads, row_count = weights_t.shape
+    key_count, depth = idx_all.shape
+    return pl.pallas_call(
+        logits_kernel,
+        out_shape=(
+            jax.ShapeDtypeStruct((row_count, key_count), jnp.float32),
+            jax.ShapeDtypeStruct((gheads, row_count, depth), jnp.bfloat16),
+        ),
+        in_specs=[pl.BlockSpec(memory_space=VMEM)] * 3,
+        out_specs=(pl.BlockSpec(memory_space=VMEM),) * 2,
+        scratch_shapes=[
+            VMEM((row_count * gheads, depth), jnp.float32),
+            VMEM((key_count, row_count), jnp.float32),
+        ],
+        name="index_forward",
+    )(index_flat, weights_t, idx_all)
+
+
+def forward_kernel(vis_ref, lat_ref, lk_ref, target_ref, bias, total):
     block, width, row_count = lat_ref.shape
-    gheads = w_ref.shape[0]
     key_count = lk_ref.shape[0]
-    depth = ik_ref.shape[1]
     step = pl.program_id(0)
     c = mla_scale * LOG2E
 
@@ -139,28 +181,6 @@
     def _():
         ids = lax.broadcasted_iota(jnp.int32, (key_count, row_count), 0)
         bias[...] = jnp.where(ids < vis_ref[...], 0.0, neg_fill)
-        wide[...] = idx_ref[...].astype(jnp.float32)
-        total[...] = jnp.zeros_like(total)
-        scale = float(depth) ** (-0.5) * INDEX_HEADS ** (-0.5)
-
-        def pair(number, _):
-            g = number * 2
-            parts = [wide[pl.ds(g + j, row_count, stride=gheads), :].astype(jnp.bfloat16) for j in range(2)]
-            for j in range(2):
-                split_ref[g + j] = parts[j]
-            products = lax.dot_general(
-                ik_ref[...], jnp.concatenate(parts, axis=0), (((1,), (1,)), ((), ())),
-                preferred_element_type=jnp.float32,
-            )
-            w = w_ref[pl.ds(g, 2), :] * scale
-            total[...] += (
-                jnp.maximum(products[:, :row_count], 0.0) * w[0:1]
-                + jnp.maximum(products[:, row_count:], 0.0) * w[1:2]
-            )
-            return 0
-
-        lax.fori_loop(0, gheads // 2, pair, 0)
-        logit_ref[...] = total[...].T
         total[...] = jnp.zeros_like(total)
 
     def scores_of(j):
@@ -185,44 +205,36 @@
         target_ref[...] = total[...].T
 
 
-def forward(latent_t, index_flat, weights_t, visible, lat_all, idx_all, block=8):
+def forward(latent_t, visible, lat_all, block=8):
     heads, width, row_count = latent_t.shape
-    gheads = weights_t.shape[0]
-    key_count, depth = idx_all.shape
+    key_count = lat_all.shape[0]
     whole = lambda *shape: pl.BlockSpec(shape, lambda i: (0,) * len(shape))
     return pl.pallas_call(
         forward_kernel,
-        out_shape=(
-            jax.ShapeDtypeStruct((row_count, key_count), jnp.float32),
-            jax.ShapeDtypeStruct((row_count, key_count), jnp.float32),
-            jax.ShapeDtypeStruct((gheads, row_count, depth), jnp.bfloat16),
-        ),
+        out_shape=jax.ShapeDtypeStruct((row_count, key_count), jnp.float32),
         grid=(heads // block,),
         in_specs=[
             whole(1, row_count),
             pl.BlockSpec((block, width, row_count), lambda i: (i, 0, 0)),
-            whole(row_count * gheads, depth),
-            whole(gheads, row_count),
             whole(key_count, width),
-            whole(key_count, depth),
-        ],
-        out_specs=(
-            whole(row_count, key_count),
-            whole(row_count, key_count),
-            whole(gheads, row_count, depth),
-        ),
-        scratch_shapes=[
-            VMEM((row_count * gheads, depth), jnp.float32),
+        ],
+        out_specs=whole(row_count, key_count),
+        scratch_shapes=[
             VMEM((key_count, row_count), jnp.float32),
             VMEM((key_count, row_count), jnp.float32),
         ],
-        name="forward_rows",
-    )(visible, latent_t, index_flat, weights_t, lat_all, idx_all)
-
-
-def exchange_kernel(nh, logit_ref, target_ref, vis_ref, slope_ref, logit_got, target_got, target_out, part, got, ss, rs):
+        cost_estimate=pl.CostEstimate(
+            flops=2 * heads * width * row_count * key_count,
+            bytes_accessed=2 * heads * width * row_count,
+            transcendentals=heads * row_count * key_count,
+        ),
+        name="latent_forward",
+    )(visible, latent_t, lat_all)
+
+
+def exchange_kernel(nh, logit_ref, target_ref, vis_ref, slope_ref, target_got, target_out, part, got, ss, rs):
     me = lax.axis_index("head")
-    share = logit_ref.shape[0] // nh
+    share = logit_ref.shape[0]
 
     def rows_of(owner):
         return pl.ds(pl.multiple_of(owner * share, share), share)
@@ -235,17 +247,11 @@
         pl.semaphore_signal(barrier, inc=1, device_id={"head": peer}, device_id_type=MESH)
     target_out[...] = target_ref[...].astype(jnp.bfloat16)
     pl.semaphore_wait(barrier, nh - 1)
-    first, second, third = [], [], []
-    for k, peer in enumerate(peers):
-        first.append(remote(logit_ref.at[rows_of(peer), :], logit_got.at[k], ss.at[0, k], rs.at[0, k], {"head": peer}))
-        first[-1].start()
+    second, third = [], []
     for k, peer in enumerate(peers):
         second.append(remote(target_out.at[rows_of(peer), :], target_got.at[k], ss.at[1, k], rs.at[1, k], {"head": peer}))
         second[-1].start()
-    logits = logit_ref[mine, :]
-    for k in range(nh - 1):
-        first[k].wait_recv()
-        logits = logits + logit_got[k]
+    logits = logit_ref[...]
     ids = lax.broadcasted_iota(jnp.int32, logits.shape, 1)
     logits = jnp.where(ids < vis_ref[mine, :], logits, neg_fill)
     weights = jnp.exp(logits - jnp.max(logits, axis=1, keepdims=True))
@@ -263,12 +269,12 @@
     for k, source in enumerate(sources):
         third[k].wait_recv()
         slope_ref[rows_of(source), :] = got[k].astype(jnp.float32)
-    for copy in first + second + third:
+    for copy in second + third:
         copy.wait_send()
 
 
 def exchange(nh, logits, targets, visible):
-    row_count, key_count = logits.shape
+    row_count, key_count = targets.shape
     share = row_count // nh
     dma = pltpu.SemaphoreType.DMA
     return pl.pallas_call(
@@ -277,7 +283,6 @@
         in_specs=[pl.BlockSpec(memory_space=VMEM)] * 3,
         out_specs=pl.BlockSpec(memory_space=VMEM),
         scratch_shapes=[
-            VMEM((nh - 1, share, key_count), jnp.float32),
             VMEM((nh - 1, share, key_count), jnp.bfloat16),
             VMEM((row_count, key_count), jnp.bfloat16),
             VMEM((share, key_count), jnp.bfloat16),
@@ -425,15 +430,17 @@
     row_count, gheads, depth = index_queries.shape
     weights_t = head_weights.T
     lat_all, idx_all = gather_keys(n, latent_keys, index_keys)
-    logits, targets, split = forward(
-        jnp.transpose(latent_queries, (1, 2, 0)),
-        index_queries.reshape(row_count * gheads, depth),
-        weights_t,
-        visible.reshape(1, row_count),
-        lat_all,
-        idx_all,
+    logits, split = index_forward(index_queries.reshape(row_count * gheads, depth), weights_t, idx_all)
+    me = lax.axis_index("head")
+    share = row_count // nh
+    mine = lax.dynamic_slice_in_dim(logits, me * share, share, 0)
+    for k in range(1, nh):
+        leaving = lax.dynamic_slice_in_dim(logits, (me + k) % nh * share, share, 0)
+        mine = mine + lax.ppermute(leaving, "head", [(i, (i + k) % nh) for i in range(nh)])
+    targets = forward(
+        jnp.transpose(latent_queries, (1, 2, 0)), visible.reshape(1, row_count), lat_all
     )
-    slope = exchange(nh, logits, targets, visible.reshape(row_count, 1))
+    slope = exchange(nh, mine, targets, visible.reshape(row_count, 1))
     query_grad, weight_grad, term = backward(split, weights_t, idx_all, slope)
     key_grad = owner_sum(n, nh, term)
     return query_grad.reshape(row_count, gheads, depth), weight_grad.T, key_grad

time: 102 us -> 100 us (0.980)
  Pallas kernels: 99 us -> 93.9 us
  starting transfers between devices: 0 us -> 1.56 us
    pallas_call x1, Pallas kernels: 18.3 us -> 11 us  [exchange(): pl.pallas_call(functools.partial(exchange_kernel, nh), out_shape=jax.Shap...]
    ppermute x0 -> x1, starting transfers between devices: none -> 1.56 us  [body(): lax.ppermute(leaving, 'head', [(i, (i + k) % nh) for i in range(nh)])]
    pallas_call x1 -> x2, Pallas kernels: 33.7 us -> 34.8 us  [the longest x1 26.7 us: forward(): pl.pallas_call(forward_kernel, out_shape=jax.ShapeDtypeStruct((row_count,...]
  transfers between devices with their start and end apart: 0 -> 1, of which waited for: 0 -> 0; matrix products, arithmetic and copies ran while one was open for 0% -> 1% of each run, Pallas kernels for 0% -> 27%
where the time goes in v3:
time: 100 us; the launch traced here: 99.9 us
  Pallas kernels  93.9 us (94%)
  local copies, waits for them, and re-layouts  3.08 us (3%)
  starting transfers between devices  1.56 us (2%)
    pallas_call x1, Pallas kernels, forward(): pl.pallas_call(forward_kernel, out_shape=jax.ShapeDtypeStruct((row_count,...  26.7 us
    pallas_call x1, Pallas kernels, gather_keys(): pl.pallas_call(functools.partial(gather_kernel, n), out_shape=(jax.ShapeD...  22.3 us
    pallas_call x1, Pallas kernels, owner_sum(): pl.pallas_call(functools.partial(owner_kernel, n, nh), out_shape=jax.Shap...  14.4 us
    pallas_call x1, Pallas kernels, backward(): pl.pallas_call(backward_kernel, out_shape=(jax.ShapeDtypeStruct((row_coun...  11.3 us
    pallas_call x1, Pallas kernels, exchange(): pl.pallas_call(functools.partial(exchange_kernel, nh), out_shape=jax.Shap...  11 us
    pallas_call x1, Pallas kernels, index_forward(): pl.pallas_call(logits_kernel, out_shape=(jax.ShapeDtypeStruct((row_count,...  8.05 us
  transfers between devices with their start and end apart: 1, of which 0 were waited for; matrix products, arithmetic and copies ran while one was open for 1% of the time, Pallas kernels for 27%

profile of v3, /device:TPU:0, one launch (start us, length us, event | category | flops | bytes accessed | tf_op | source)
XLA Modules:
  0.0 99.9 jit_solution(14436555051154475440)
XLA Ops:
  0.6 22.3 %gather_keys.1 = (bf16[1024,576]{1,0:T(8,128)(2,1)}, bf16[1024,128]{1,0:T(8,128)(2,1)}) custom-call(bf16[64,576]{1,0:T(8,128)(2,1)} %lat_ref.1, bf16[64,128]{1,0:T(8,128)(2,1)} %idx_ref.1), custom_call_target="tpu_custom_call" | custom-call | tf_op jit(solution)/shard_map/gather_keys/pallas_call | solution.py:109
  23.0 8.0 %index_forward.1 = (f32[128,1024]{1,0:T(8,128)}, bf16[32,128,128]{2,1,0:T(8,128)(2,1)}) custom-call(bf16[4096,128]{1,0:T(8,128)(2,1)} %bitcast.7, f32[32,128]{1,0:T(8,128)} %bitcast.8, bf16[1024,128]{1,0:T(8,128)(2,1)} %get-tuple-element.10.ik_ref), custom_call_target="tpu_custom_call" | custom-call | tf_op jit(solution)/shard_map/index_forward/pallas_call | solution.py:158
  31.0 1.0 constant_dynamic-slice_fusion
  32.0 1.6 %collective-permute-start = (f32[64,1024]{1,0:T(8,128)S(1)}, f32[64,1024]{1,0:T(8,128)S(1)}, u32[]{:S(2)}, u32[]{:S(2)}) collective-permute-start(f32[64,1024]{1,0:T(8,128)S(1)} %constant_dynamic-slice_fusion), channel_id=1, source_target_pairs={{0,1},{1,0},{2,3},{3,2},{4,5},{5,4},{6,7},{7,6},{8,9},{9,8},{10,11... | collective-permute-start | bytes 786440 | tf_op jit(solution)/shard_map/ppermute | solution.py:439
  33.6 0.0 copy-start.1
  33.6 0.0 copy-start
  33.6 26.7 %latent_forward.1.target_ref = f32[128,1024]{1,0:T(8,128)} custom-call(s32[1,128]{1,0:T(1,128)} %bitcast.10, bf16[64,576,128]{2,1,0:T(8,128)(2,1)} %bitcast.12, bf16[1024,576]{1,0:T(8,128)(2,1)} %get-tuple-element.13.lk_ref), custom_call_target="tpu_custom_call" | custom-call | flops 9663676416 | bytes 9437184 | tf_op jit(solution)/shard_map/latent_forward/pallas_call | solution.py:212
  60.3 0.0 copy-done.1
  60.3 0.7 copy.9.vis_ref
  61.0 0.0 collective-permute-done
  61.0 0.0 copy-done
  61.0 0.7 dynamic-slice_add_fusion.logit_ref
  61.8 11.0 %head_exchange.1.slope_ref = f32[128,1024]{1,0:T(8,128)} custom-call(f32[64,1024]{1,0:T(8,128)} %dynamic-slice_add_fusion.logit_ref, f32[128,1024]{1,0:T(8,128)} %latent_forward.1.target_ref, s32[128,1]{1,0:T(8,128)} %copy.9.vis_ref), custom_call_target="tpu_custom_call" | custom-call | tf_op jit(solution)/shard_map/head_exchange/pallas_call | solution.py:280
  72.8 11.3 %index_backward.1 = (bf16[4096,128]{1,0:T(8,128)(2,1)}, f32[32,128]{1,0:T(8,128)}, bf16[1024,128]{1,0:T(8,128)(2,1)}) custom-call(bf16[32,128,128]{2,1,0:T(8,128)(2,1)} %get-tuple-element.11.split_ref, f32[32,128]{1,0:T(8,128)} %bitcast.9, bf16[1024,128]{1,0:T(8,128)(2,1)} %get-tuple-element.10.ik_ref, f32[128,1024]{1,0:T(8,128)} %head_exchange.1.slope_ref), custom_call_target="tpu_custom_call" | custom-call | tf_op jit(solution)/shard_map/index_backward/pallas_call | solution.py:342
  84.1 14.4 %owner_sum.1 = f32[64,128]{1,0:T(8,128)} custom-call(bf16[1024,128]{1,0:T(8,128)(2,1)} %get-tuple-element.16.term_ref), custom_call_target="tpu_custom_call" | custom-call | tf_op jit(solution)/shard_map/owner_sum/pallas_call | solution.py:413
  98.6 1.4 %copy.11 = f32[64,128]{1,0:T(8,128)} copy(f32[64,128]{1,0:T(8,128)} %owner_sum.1) | data formatting | bytes 65536
Async XLA Ops:
  32.0 29.0 %collective-permute-start = (f32[64,1024]{1,0:T(8,128)S(1)}, f32[64,1024]{1,0:T(8,128)S(1)}, u32[]{:S(2)}, u32[]{:S(2)}) collective-permute-start(f32[64,1024]{1,0:T(8,128)S(1)} %constant_dynamic-slice_fusion), channel_id=1, source_target_pairs={{0,1},{1,0},{2,3},{3,2},{4,5},{5,4},{6,7},{7,6},{8,9},{9,8},{10,11... | collective-permute-start | bytes 786440 | tf_op jit(solution)/shard_map/ppermute | solution.py:439
  33.6 26.7 %copy-start.1 = (s32[128]{0:T(128)S(1)}, s32[128]{0:T(128)}, u32[]{:S(2)}) copy-start(s32[128]{0:T(128)} %param.11) | copy-start | bytes 1540
  33.6 27.5 %copy-start = (f32[128,1024]{1,0:T(8,128)S(1)}, f32[128,1024]{1,0:T(8,128)}, u32[]{:S(2)}) copy-start(f32[128,1024]{1,0:T(8,128)} %get-tuple-element.12) | copy-start | bytes 1572868
